TPU v7x, 32 devices: a whole 2x2x4 slice. The times are simulated.
32 devices in a mesh: facet: 8 (over y, x, core), col: 4 (over z).
Axes of the slice: x: 2, y: 2, z: 4, core: 2. Of those that a mesh axis runs over, the one named last changes fastest.
Arguments:
- facets: float32 [2, 8, 24, 2, 4096], P(None, 'facet', None, None, 'col'), may hold values from -6 to 6
- facet_x: int32 [8], P('facet'), may hold values from 0 to 32767
- facet_y: int32 [2], replicated, may hold values from 0 to 32767
- col_u: int32 [8], replicated, may hold values from 0 to 32767
- slot_col: int32 [4, 8], P('col'), may hold values from 0 to 1
- slot_v: int32 [4, 8], P('col'), may hold values from 0 to 32767
Outputs:
- subgrids: float32 [4, 8, 512, 1024], P('col', 'facet')
Inputs may be any that keep to these rules, and one draw needn't show every extreme that they name: `col_u`: offset in the image. `slot_col`: the subgrid's column is owner * 2 + this value. `slot_v`: offset in the image.
All inputs are finite; a program needn't handle non-finite values.
Results may differ from a plain program's by a relative error of at most 0.0003.
Values sent between devices are 32-bit elements; how exact they have to be, the bound alone decides.
A program may use at most 128 MiB of HBM per device.

v0:
```python
import math
import jax
import jax.numpy as jnp
from jax import lax
from jax.sharding import PartitionSpec as P

FS = 4096
SG = 512
COLS_DEV = 2
SLOTS = 1


def mulmod(first_factor, second_factor, modulus):
    upper = first_factor * (second_factor // 512) % modulus
    return (upper * 512 + first_factor * (second_factor % 512)) % modulus


def column_part(real_part, imag_part, shifted, table, col_u, img, count):
    turn = 2.0 * math.pi / img
    column_angle = mulmod(col_u[:, None], shifted[None, :], img).astype(jnp.float32) * turn
    cosine = jnp.cos(column_angle)[:, None, :]
    sine = jnp.sin(column_angle)[:, None, :]
    turned_real = real_part[None] * cosine + imag_part[None] * sine
    turned_imag = imag_part[None] * cosine - real_part[None] * sine
    local_rows = real_part.shape[0]
    width = real_part.shape[1]
    stacked = jnp.stack([turned_real, turned_imag]).reshape(-1, width)
    product = jnp.dot(
        stacked, table, precision=lax.Precision.HIGHEST, preferred_element_type=jnp.float32
    )
    product = product.reshape(2, count, local_rows, 2 * SG)
    from_real = product[0]
    from_imag = product[1]
    real_out = from_real[..., :SG] + from_imag[..., SG:]
    imag_out = from_imag[..., :SG] - from_real[..., SG:]
    return jnp.concatenate([real_out, imag_out], axis=-1)


def slot_term(owned, row_cells, img, column, shift_v):
    turn = 2.0 * math.pi / img
    v_cells = (shift_v + jnp.arange(SG, dtype=jnp.int32)) % img
    angle = mulmod(v_cells[:, None], row_cells[None, :], img).astype(jnp.float32) * turn
    cosine = jnp.cos(angle)
    sine = jnp.sin(angle)
    chosen = lax.dynamic_index_in_dim(owned, column, 0, keepdims=False)
    first = jnp.dot(
        cosine, chosen, precision=lax.Precision.HIGHEST, preferred_element_type=jnp.float32
    )
    second = jnp.dot(
        sine, chosen, precision=lax.Precision.HIGHEST, preferred_element_type=jnp.float32
    )
    real_out = first[:, :SG] + second[:, SG:]
    imag_out = first[:, SG:] - second[:, :SG]
    return jnp.concatenate([real_out, imag_out], axis=-1)


def per_device(facets, facet_x, facet_y, col_u, slot_col, slot_v):
    width = facets.shape[-1]
    band_rows = facets.shape[2]
    img = FS * lax.axis_size("facet")
    turn = 2.0 * math.pi / img
    x_start = lax.axis_index("col") * width
    real_part = facets[:, 0, :, 0, :].reshape(-1, width)
    imag_part = facets[:, 0, :, 1, :].reshape(-1, width)
    shifted = (facet_x[0] + x_start + jnp.arange(width, dtype=jnp.int32)) % img
    u_cells = jnp.arange(SG, dtype=jnp.int32)
    table_angle = mulmod(u_cells[None, :], shifted[:, None], img).astype(jnp.float32) * turn
    table = jnp.concatenate([jnp.cos(table_angle), jnp.sin(table_angle)], axis=1)
    owned = lax.psum_scatter(
        column_part(
            real_part, imag_part, shifted, table, col_u, img, COLS_DEV * lax.axis_size("col")
        ),
        "col",
        scatter_dimension=0,
        tiled=True,
    )
    total_rows = owned.shape[1]
    row_ids = jnp.arange(total_rows, dtype=jnp.int32)
    y_start = jnp.where(row_ids // band_rows == 0, facet_y[0], facet_y[1])
    row_cells = (y_start + row_ids % band_rows) % img
    scale = 1.0 / math.sqrt(2.0 * FS * band_rows * lax.axis_size("facet"))
    owner_cols = slot_col[0]
    owner_shift = slot_v[0]
    merged = lax.psum(owned, "facet")

    def own_slot(slot_id):
        return slot_term(merged, row_cells, img, owner_cols[slot_id], owner_shift[slot_id])

    first_slot = lax.axis_index("facet") * SLOTS
    summed = lax.map(own_slot, first_slot + jnp.arange(SLOTS, dtype=jnp.int32))
    return (summed * scale)[None]


def solution(mesh):
    placed = (
        P(None, "facet", None, None, "col"),
        P("facet"),
        P(),
        P(),
        P("col", None),
        P("col", None),
    )
    return jax.shard_map(
        per_device,
        mesh=mesh,
        in_specs=placed,
        out_specs=P("col", "facet", None, None),
        check_vma=False,
    )
```

profile of v0, /device:TPU:0, one launch (start us, length us, event | category | flops | bytes accessed | tf_op | source)
XLA Modules:
  0.0 140.9 jit_solution(5407549524900106008)
XLA Ops:
  6.5 0.0 reduce-scatter.2.cloned.1.call-start
  7.2 0.0 copy-start.3
  7.2 0.0 copy-start
  7.2 9.3 %fusion.16 = (f32[1024,512]{1,0:T(8,128)S(1)}, f32[1024,512]{1,0:T(8,128)S(1)}) fusion(s32[1024]{0:T(1024)S(1)} %get-tuple-element.42, s32[1024]{0:T(1024)S(1)} %get-tuple-element.43), kind=kLoop, calls=%fused_computation.29 | loop fusion | flops 14680064 | bytes 4202496 | tf_op jit(solution)/shard_map/cos | solution.py:68
  16.5 0.0 copy-done.3
  16.5 0.2 fusion.40
  16.8 0.0 copy-done
  16.8 0.3 fusion.62
  17.2 0.4 multiply_add_fusion
  17.6 0.4 pad_maximum_fusion
  18.0 10.6 %fusion = f32[768,1024]{1,0:T(8,128)S(1)} fusion(f32[768,1024]{1,0:T(8,128)S(1)} %bitcast.23, f32[1024,512]{1,0:T(8,128)S(1)} %get-tuple-element.39, f32[1024,512]{1,0:T(8,128)S(1)} %get-tuple-element.38), kind=kOutput, calls=%fused_computation | convolution fusion | flops 9664724992 | bytes 10485760 | tf_op jit(solution)/shard_map/dot_general | solution.py:28
  28.6 0.4 fusion.61
  29.0 0.3 slice_add_fusion.1
  29.3 0.0 copy-start.4
  29.4 0.0 copy-start.5
  29.4 0.0 copy-start.2
  29.4 1.3 pad_maximum_fusion.1
  30.7 0.0 reduce-scatter.2.cloned.1.call-update
  30.7 0.3 all-reduce.2.cloned.1.call-start
  31.0 0.0 copy-done.4
  31.0 0.0 copy-done.5
  31.0 0.6 constant_dynamic-slice_fusion
  33.5 0.0 copy-done.2
  33.5 0.6 fusion.63
  34.1 34.9 %reduce-scatter.2.cloned.1.call-done = f32[2,48,1024]{2,1,0:T(8,128)} async-done(((f32[8,48,1024]{2,1,0:T(8,128)}), f32[2,48,1024]{2,1,0:T(8,128)}) %reduce-scatter.2.cloned.1.call-update) | async-done | bytes 393232 | tf_op jit(solution)/shard_map/reduce_scatter | solution.py:69
  69.0 0.0 all-reduce.2.cloned.1.call-update
  69.0 1.2 and_select_fusion
  70.2 0.6 add_select_fusion.9
  70.9 54.4 %all-reduce.2.cloned.1.call-done = f32[2,48,1024]{2,1,0:T(8,128)} async-done(((f32[2,48,1024]{2,1,0:T(8,128)}), f32[2,48,1024]{2,1,0:T(8,128)}) %all-reduce.2.cloned.1.call-update) | async-done | bytes 393232 | tf_op jit(solution)/shard_map/psum | solution.py:84
  125.3 0.0 copy-start.1
  125.3 3.8 %fusion.25 = f32[512,1024]{1,0:T(8,128)S(1)} fusion(f32[2,48,1024]{2,1,0:T(8,128)} %all-reduce.2.cloned.1.call-done, s32[]{:T(128)S(6)} %select_n.215, s32[48]{0:T(128)S(1)} %get-tuple-element.44, s32[48]{0:T(128)S(1)} %get-tuple-element.45, s32[512]{0:T(512)S(1)} %add_select_fusion.9), kind=kOutput, calls=%fused_computation.48 | convolution fusion | flops 302678016 | bytes 2296196 | tf_op jit(solution)/shard_map/while/body/eval_jaxpr/dot_general | solution.py:46
  129.2 0.0 copy-done.1
  129.2 2.8 %fusion.23 = f32[512,1024]{1,0:T(8,128)S(1)} fusion(f32[2,48,1024]{2,1,0:T(8,128)S(1)} %copy-done.1, s32[]{:T(128)S(6)} %select_n.215, s32[48]{0:T(128)S(1)} %get-tuple-element.44, s32[48]{0:T(128)S(1)} %get-tuple-element.45, s32[512]{0:T(512)S(1)} %add_select_fusion.9), kind=kOutput, calls=%fused_computation.46 | convolution fusion | flops 302678016 | bytes 2296836 | tf_op jit(solution)/shard_map/while/body/eval_jaxpr/dot_general | solution.py:49
  132.0 0.5 fusion.14
  132.5 1.5 %maximum_multiply_fusion = f32[1,1,512,1024]{3,2,1,0:T(8,128)} fusion(f32[1,1,512,512]{3,2,1,0:T(8,128)S(1)} %get-tuple-element.18, f32[1,1,512,512]{3,2,1,0:T(8,128)S(1)} %get-tuple-element.17), kind=kLoop, calls=%fused_computation.17 | loop fusion | flops 1048576 | bytes 4194304 | tf_op jit(solution)/shard_map/mul | solution.py:91
  (3 shorter events, 0.1 us)
Async XLA Ops:
  6.5 62.5 %reduce-scatter.2.cloned.1.call-start = ((), (), s32[]{:S(2)}) async-start(), calls=%async_computation.1 | async-start | bytes 1966080 | tf_op jit(solution)/shard_map/reduce_scatter | solution.py:69
  7.2 9.3 %copy-start.3 = (s32[8]{0:T(128)S(1)}, s32[8]{0:T(128)}, u32[]{:S(2)}) copy-start(s32[8]{0:T(128)} %param.9) | copy-start | bytes 100
  7.2 9.6 %copy-start = (f32[2,1,24,2,1024]{4,3,2,1,0:T(2,128)S(1)}, f32[2,1,24,2,1024]{4,3,2,1,0:T(2,128)}, u32[]{:S(2)}) copy-start(f32[2,1,24,2,1024]{4,3,2,1,0:T(2,128)} %param.6) | copy-start | bytes 1179652
  29.3 1.6 %copy-start.4 = (s32[1,8]{1,0:T(1,128)S(1)}, s32[1,8]{1,0:T(1,128)}, u32[]{:S(2)}) copy-start(s32[1,8]{1,0:T(1,128)} %param.10) | copy-start | bytes 100
  29.4 1.6 %copy-start.5 = (s32[1,8]{1,0:T(1,128)S(1)}, s32[1,8]{1,0:T(1,128)}, u32[]{:S(2)}) copy-start(s32[1,8]{1,0:T(1,128)} %param.11) | copy-start | bytes 100
  29.4 4.1 %copy-start.2 = (s32[2]{0:T(128)S(1)}, s32[2]{0:T(128)}, u32[]{:S(2)}) copy-start(s32[2]{0:T(128)} %param.8) | copy-start | bytes 28
  30.7 94.6 %all-reduce.2.cloned.1.call-start = ((), (), s32[]{:S(2)}) async-start(), calls=%async_computation.2 | async-start | bytes 786432 | tf_op jit(solution)/shard_map/psum | solution.py:84
  125.3 3.8 %copy-start.1 = (f32[2,48,1024]{2,1,0:T(8,128)S(1)}, f32[2,48,1024]{2,1,0:T(8,128)}, u32[]{:S(2)}) copy-start(f32[2,48,1024]{2,1,0:T(8,128)} %all-reduce.2.cloned.1.call-done) | copy-start | bytes 1179652
Sparse Core Ops, SparseCore 0:
  30.8 38.1 reduce-scatter.1
  72.1 53.2 all-reduce.1
where the time goes:
time: 141 us
  waiting for transfers between devices  89.4 us (63%)
  matrix products  17.2 us (12%)
  between operations  16.2 us (11%)
  other arithmetic  15.9 us (11%)
  local copies, waits for them, and re-layouts  1.98 us (1%)
    psum x1, waiting for transfers between devices, per_device(): merged = lax.psum(owned, 'facet')  54.4 us
    reduce_scatter x1, waiting for transfers between devices, per_device(): lax.psum_scatter(column_part(real_part, imag_part, shifted, table, col_u,...  34.9 us
    dot_general x1, matrix products, column_part(): jnp.dot(stacked, table, precision=lax.Precision.HIGHEST, preferred_elemen...  10.6 us
    cos x1, other arithmetic, per_device(): jnp.cos(table_angle)  9.29 us
    dot_general x1, matrix products, slot_term(): jnp.dot(cosine, chosen, precision=lax.Precision.HIGHEST, preferred_elemen...  3.81 us
    dot_general x1, matrix products, slot_term(): jnp.dot(sine, chosen, precision=lax.Precision.HIGHEST, preferred_element_...  2.82 us
  transfers between devices with their start and end apart: 2, of which 2 were waited for; matrix products, arithmetic and copies ran while one was open for 2% of the time, Pallas kernels for 0%

commit v1 on v0

--- a/solution.py
+++ b/solution.py
@@ -8,6 +8,15 @@
 SG = 512
 COLS_DEV = 2
 SLOTS = 1
+
+
+def add_in_pairs(x, axis):
+    size = lax.axis_size(axis)
+    total, far = (x, 1)
+    while far < size:
+        total = total + lax.ppermute(total, axis, [(i, i ^ far) for i in range(size)])
+        far = 2 * far
+    return total
 
 
 def mulmod(first_factor, second_factor, modulus):
@@ -81,7 +90,7 @@
     scale = 1.0 / math.sqrt(2.0 * FS * band_rows * lax.axis_size("facet"))
     owner_cols = slot_col[0]
     owner_shift = slot_v[0]
-    merged = lax.psum(owned, "facet")
+    merged = add_in_pairs(owned, "facet")
 
     def own_slot(slot_id):
         return slot_term(merged, row_cells, img, owner_cols[slot_id], owner_shift[slot_id])

time: 141 us -> 109 us (0.77)
  waiting for transfers between devices: 89.4 us -> 53.6 us
  starting transfers between devices: 0.26 us -> 3.1 us
    psum x1 -> x0, waiting for transfers between devices: 54.4 us -> none  [per_device(): merged = lax.psum(owned, 'facet')]
    ppermute x0 -> x3, waiting for transfers between devices: none -> 15.3 us  [add_in_pairs(): lax.ppermute(total, axis, [(i, i ^ far) for i in range(size)])]
    reduce_scatter x1, waiting for transfers between devices: 34.9 us -> 38.3 us  [per_device(): lax.psum_scatter(column_part(real_part, imag_part, shifted, table, col_u,...]
    ppermute x0 -> x3, starting transfers between devices: none -> 3.1 us  [add_in_pairs(): lax.ppermute(total, axis, [(i, i ^ far) for i in range(size)])]
  transfers between devices with their start and end apart: 2 -> 4, of which waited for: 2 -> 4; matrix products, arithmetic and copies ran while one was open for 2% -> 3% of each run, Pallas kernels for 0% -> 0%
where the time goes in v1:
time: 109 us; the launch traced here: 108 us
  waiting for transfers between devices  53.6 us (49%)
  other arithmetic  17 us (16%)
  matrix products  16.4 us (15%)
  between operations  16.1 us (15%)
  starting transfers between devices  3.1 us (3%)
  local copies, waits for them, and re-layouts  2.02 us (2%)
    reduce_scatter x1, waiting for transfers between devices, per_device(): lax.psum_scatter(column_part(real_part, imag_part, shifted, table, col_u,...  38.3 us
    ppermute x3, waiting for transfers between devices, add_in_pairs(): lax.ppermute(total, axis, [(i, i ^ far) for i in range(size)])  15.3 us
    dot_general x1, matrix products, column_part(): jnp.dot(stacked, table, precision=lax.Precision.HIGHEST, preferred_elemen...  10.6 us
    cos x1, other arithmetic, per_device(): jnp.cos(table_angle)  9.29 us
    ppermute x3, starting transfers between devices, add_in_pairs(): lax.ppermute(total, axis, [(i, i ^ far) for i in range(size)])  3.1 us
    dot_general x1, matrix products, slot_term(): jnp.dot(sine, chosen, precision=lax.Precision.HIGHEST, preferred_element_...  3.05 us
    dot_general x1, matrix products, slot_term(): jnp.dot(cosine, chosen, precision=lax.Precision.HIGHEST, preferred_elemen...  2.82 us
  transfers between devices with their start and end apart: 4, of which 4 were waited for; matrix products, arithmetic and copies ran while one was open for 3% of the time, Pallas kernels for 0%

profile of v1, /device:TPU:0, one launch (start us, length us, event | category | flops | bytes accessed | tf_op | source)
XLA Modules:
  0.0 108.3 jit_solution(2230050056031637530)
XLA Ops:
  6.5 0.0 reduce-scatter.2.cloned.1.call-start
  7.2 0.0 copy-start.2
  7.2 0.0 copy-start
  7.2 9.3 %fusion.16 = (f32[1024,512]{1,0:T(8,128)S(1)}, f32[1024,512]{1,0:T(8,128)S(1)}) fusion(s32[1024]{0:T(1024)S(1)} %get-tuple-element.42, s32[1024]{0:T(1024)S(1)} %get-tuple-element.43), kind=kLoop, calls=%fused_computation.29 | loop fusion | flops 14680064 | bytes 4202496 | tf_op jit(solution)/shard_map/cos | solution.py:77
  16.5 0.0 copy-done.2
  16.5 0.2 fusion.39
  16.8 0.0 copy-done
  16.8 0.3 fusion.61
  17.2 0.4 multiply_add_fusion
  17.6 0.4 pad_maximum_fusion
  18.0 10.6 %fusion = f32[768,1024]{1,0:T(8,128)S(1)} fusion(f32[768,1024]{1,0:T(8,128)S(1)} %bitcast.22, f32[1024,512]{1,0:T(8,128)S(1)} %get-tuple-element.39, f32[1024,512]{1,0:T(8,128)S(1)} %get-tuple-element.38), kind=kOutput, calls=%fused_computation | convolution fusion | flops 9664724992 | bytes 10485760 | tf_op jit(solution)/shard_map/dot_general | solution.py:37
  28.6 0.4 fusion.60
  29.0 0.3 slice_add_fusion.1
  29.3 1.3 %pad_maximum_fusion.1 = f32[8,48,1024]{2,1,0:T(8,128)} fusion(f32[8,48,512]{2,1,0:T(8,128)S(1)} %get-tuple-element.20, f32[8,48,512]{2,1,0:T(8,128)S(1)} %get-tuple-element.19), kind=kLoop, calls=%fused_computation.21 | loop fusion | flops 393216 | bytes 3145728 | tf_op jit(solution)/shard_map/concatenate | solution.py:45
  30.6 0.0 copy-start.3
  30.6 0.0 copy-start.4
  30.6 0.0 copy-start.1
  30.6 0.0 reduce-scatter.2.cloned.1.call-update
  30.7 38.3 %reduce-scatter.2.cloned.1.call-done = f32[2,48,1024]{2,1,0:T(8,128)} async-done(((f32[8,48,1024]{2,1,0:T(8,128)}), f32[2,48,1024]{2,1,0:T(8,128)}) %reduce-scatter.2.cloned.1.call-update) | async-done | bytes 393232 | tf_op jit(solution)/shard_map/reduce_scatter | solution.py:78
  69.0 0.0 collective-permute-start
  69.0 1.9 %collective-permute-done = f32[2,48,1024]{2,1,0:T(8,128)S(1)} collective-permute-done((f32[2,48,1024]{2,1,0:T(8,128)}, f32[2,48,1024]{2,1,0:T(8,128)S(1)}, u32[]{:S(2)}, u32[]{:S(2)}) %collective-permute-start) | collective-permute-done | bytes 393248 | tf_op jit(solution)/shard_map/ppermute | solution.py:17
  70.9 1.1 add.286
  71.9 1.5 %collective-permute-start.1 = (f32[2,48,1024]{2,1,0:T(8,128)S(1)}, f32[2,48,1024]{2,1,0:T(8,128)S(1)}, u32[]{:S(2)}, u32[]{:S(2)}) collective-permute-start(f32[2,48,1024]{2,1,0:T(8,128)S(1)} %add.286), channel_id=1, source_target_pairs={{0,8},{4,12},{8,0},{12,4},{16,24},{20,28},{24,16},{28,20},{1,9},{5... | collective-permute-start | bytes 1179656 | tf_op jit(solution)/shard_map/ppermute | solution.py:17
  73.5 9.7 %collective-permute-done.1 = f32[2,48,1024]{2,1,0:T(8,128)S(1)} collective-permute-done((f32[2,48,1024]{2,1,0:T(8,128)S(1)}, f32[2,48,1024]{2,1,0:T(8,128)S(1)}, u32[]{:S(2)}, u32[]{:S(2)}) %collective-permute-start.1) | collective-permute-done | bytes 393248 | tf_op jit(solution)/shard_map/ppermute | solution.py:17
  83.2 1.5 %collective-permute-start.2 = (f32[2,48,1024]{2,1,0:T(8,128)S(1)}, f32[2,48,1024]{2,1,0:T(8,128)S(1)}, u32[]{:S(2)}, u32[]{:S(2)}) collective-permute-start(f32[2,48,1024]{2,1,0:T(8,128)S(1)} %add.287), channel_id=1, source_target_pairs={{0,16},{4,20},{8,24},{12,28},{16,0},{20,4},{24,8},{28,12},{1,17},{... | collective-permute-start | bytes 1179656 | tf_op jit(solution)/shard_map/ppermute | solution.py:17
  84.8 0.0 copy-done.3
  84.8 0.0 copy-done.4
  84.8 0.7 constant_dynamic-slice_fusion
  87.4 0.0 copy-done.1
  87.4 0.6 fusion.62
  88.0 1.2 %and_select_fusion = (s32[48]{0:T(128)S(1)}, s32[48]{0:T(128)S(1)}) fusion(s32[]{:T(128)} %bitcast.2, s32[]{:T(128)} %bitcast.1), kind=kLoop, calls=%fused_computation.89 | loop fusion | flops 2160 | bytes 392 | tf_op jit(solution)/shard_map/while/body/eval_jaxpr/jit(remainder)/select_n | solution.py:24
  89.2 0.7 add_select_fusion.9
  89.9 3.7 %collective-permute-done.2 = f32[2,48,1024]{2,1,0:T(8,128)S(1)} collective-permute-done((f32[2,48,1024]{2,1,0:T(8,128)S(1)}, f32[2,48,1024]{2,1,0:T(8,128)S(1)}, u32[]{:S(2)}, u32[]{:S(2)}) %collective-permute-start.2) | collective-permute-done | bytes 393248 | tf_op jit(solution)/shard_map/ppermute | solution.py:17
  93.6 2.8 %fusion.25 = f32[512,1024]{1,0:T(8,128)S(1)} fusion(s32[48]{0:T(128)S(1)} %get-tuple-element.44, s32[48]{0:T(128)S(1)} %get-tuple-element.45, s32[512]{0:T(512)S(1)} %add_select_fusion.9, f32[2,48,1024]{2,1,0:T(8,128)S(1)} %collective-permute-done.2, s32[]{:T(128)S(6)} %select_n.215, f32[2,48,1024]{2,1,0:T(8,128)S(1)} %add.287), kind=kOutput, calls=%fused_computation.48 | convolution fusion | flops 302727168 | bytes 2493444 | tf_op jit(solution)/shard_map/while/body/eval_jaxpr/dot_general | solution.py:55
  96.4 3.1 %fusion.23 = f32[512,1024]{1,0:T(8,128)S(1)} fusion(s32[48]{0:T(128)S(1)} %get-tuple-element.44, s32[48]{0:T(128)S(1)} %get-tuple-element.45, s32[512]{0:T(512)S(1)} %add_select_fusion.9, f32[2,48,1024]{2,1,0:T(8,128)S(1)} %collective-permute-done.2, s32[]{:T(128)S(6)} %select_n.215, f32[2,48,1024]{2,1,0:T(8,128)S(1)} %add.287), kind=kOutput, calls=%fused_computation.46 | convolution fusion | flops 302727168 | bytes 2493444 | tf_op jit(solution)/shard_map/while/body/eval_jaxpr/dot_general | solution.py:58
  99.5 0.5 fusion.14
  100.0 1.5 %maximum_multiply_fusion = f32[1,1,512,1024]{3,2,1,0:T(8,128)} fusion(f32[1,1,512,512]{3,2,1,0:T(8,128)S(1)} %get-tuple-element.18, f32[1,1,512,512]{3,2,1,0:T(8,128)S(1)} %get-tuple-element.17), kind=kLoop, calls=%fused_computation.17 | loop fusion | flops 1048576 | bytes 4194304 | tf_op jit(solution)/shard_map/mul | solution.py:100
  (4 shorter events, 0.1 us)
Async XLA Ops:
  6.5 62.4 %reduce-scatter.2.cloned.1.call-start = ((), (), s32[]{:S(2)}) async-start(), calls=%async_computation.1 | async-start | bytes 1966080 | tf_op jit(solution)/shard_map/reduce_scatter | solution.py:78
  7.2 9.3 %copy-start.2 = (s32[8]{0:T(128)S(1)}, s32[8]{0:T(128)}, u32[]{:S(2)}) copy-start(s32[8]{0:T(128)} %param.9) | copy-start | bytes 100
  7.2 9.6 %copy-start = (f32[2,1,24,2,1024]{4,3,2,1,0:T(2,128)S(1)}, f32[2,1,24,2,1024]{4,3,2,1,0:T(2,128)}, u32[]{:S(2)}) copy-start(f32[2,1,24,2,1024]{4,3,2,1,0:T(2,128)} %param.6) | copy-start | bytes 1179652
  30.6 54.1 %copy-start.3 = (s32[1,8]{1,0:T(1,128)S(1)}, s32[1,8]{1,0:T(1,128)}, u32[]{:S(2)}) copy-start(s32[1,8]{1,0:T(1,128)} %param.10) | copy-start | bytes 100
  30.6 54.1 %copy-start.4 = (s32[1,8]{1,0:T(1,128)S(1)}, s32[1,8]{1,0:T(1,128)}, u32[]{:S(2)}) copy-start(s32[1,8]{1,0:T(1,128)} %param.11) | copy-start | bytes 100
  30.6 56.8 %copy-start.1 = (s32[2]{0:T(128)S(1)}, s32[2]{0:T(128)}, u32[]{:S(2)}) copy-start(s32[2]{0:T(128)} %param.8) | copy-start | bytes 28
  69.0 1.9 %collective-permute-start = (f32[2,48,1024]{2,1,0:T(8,128)}, f32[2,48,1024]{2,1,0:T(8,128)S(1)}, u32[]{:S(2)}, u32[]{:S(2)}) collective-permute-start(f32[2,48,1024]{2,1,0:T(8,128)} %reduce-scatter.2.cloned.1.call-done), channel_id=1, source_target_pairs={{0,4},{4,0},{8,12},{12,8},{16,20},{20,16},{24,28},{28,24},{1,5},{5... | collective-permute-start | bytes 1179656 | tf_op jit(solution)/shard_map/ppermute | solution.py:17
  71.9 11.2 %collective-permute-start.1 = (f32[2,48,1024]{2,1,0:T(8,128)S(1)}, f32[2,48,1024]{2,1,0:T(8,128)S(1)}, u32[]{:S(2)}, u32[]{:S(2)}) collective-permute-start(f32[2,48,1024]{2,1,0:T(8,128)S(1)} %add.286), channel_id=1, source_target_pairs={{0,8},{4,12},{8,0},{12,4},{16,24},{20,28},{24,16},{28,20},{1,9},{5... | collective-permute-start | bytes 1179656 | tf_op jit(solution)/shard_map/ppermute | solution.py:17
  83.2 10.4 %collective-permute-start.2 = (f32[2,48,1024]{2,1,0:T(8,128)S(1)}, f32[2,48,1024]{2,1,0:T(8,128)S(1)}, u32[]{:S(2)}, u32[]{:S(2)}) collective-permute-start(f32[2,48,1024]{2,1,0:T(8,128)S(1)} %add.287), channel_id=1, source_target_pairs={{0,16},{4,20},{8,24},{12,28},{16,0},{20,4},{24,8},{28,12},{1,17},{... | collective-permute-start | bytes 1179656 | tf_op jit(solution)/shard_map/ppermute | solution.py:17
Sparse Core Ops, SparseCore 0:
  30.8 38.1 reduce-scatter.1
